TPU v7x, 32 devices: a whole 2x2x4 slice. The times are simulated.
32 devices in a mesh: dp: 8 (over y, x, core), tensor: 4 (over z).
Axes of the slice: x: 2, y: 2, z: 4, core: 2. Of those that a mesh axis runs over, the one named last changes fastest.
Arguments:
- tokens: bfloat16 [32, 1024, 512], P(('dp', 'tensor')), may hold values from -6 to 6
- timestep: int32 [32], P(('dp', 'tensor')), may hold values from 0 to 999
- segment_ids: int32 [32, 1024], P('dp'), may hold values from 0 to 7, never falling along the last dimension, each value on 1 to 512 neighbouring positions
- span_lengths: int32 [32], P('dp'), may hold values from 512 to 1024
- w_qkv: float32 [3, 512, 512], P(None, 'dp', 'tensor'), may hold values from -0.25 to 0.25
- w_out_t: float32 [512, 512], P('dp', 'tensor'), may hold values from -1.5 to 1.5
- w_up: float32 [512, 2048], P('dp', 'tensor'), may hold values from -0.25 to 0.25
- w_down_t: float32 [512, 2048], P('dp', 'tensor'), may hold values from -0.125 to 0.125
- w_time: float32 [512, 512], replicated, may hold values from -0.25 to 0.25
- b_time: float32 [512], replicated, may hold values from -3 to 3
- ln1_gain: float32 [512], replicated, may hold values from 0.1 to 1.9
- ln1_bias: float32 [512], replicated, may hold values from -3 to 3
- ln2_gain: float32 [512], replicated, may hold values from 0.1 to 1.9
- ln2_bias: float32 [512], replicated, may hold values from -3 to 3
- b_up: float32 [2048], replicated, may hold values from -3 to 3
- b_down: float32 [512], replicated, may hold values from -3 to 3
- cotangent: bfloat16 [32, 1024, 512], P(('dp', 'tensor')), may hold values from -6 to 6
Outputs:
- layer_out: bfloat16 [32, 1024, 512], P(('dp', 'tensor'))
- grad_tokens: float32 [32, 1024, 512], P(('dp', 'tensor'))
- grad_w_qkv: float32 [3, 512, 512], P(None, 'dp', 'tensor')
- grad_w_out_t: float32 [512, 512], P('dp', 'tensor')
- grad_w_up: float32 [512, 2048], P('dp', 'tensor')
- grad_w_down_t: float32 [512, 2048], P('dp', 'tensor')
- grad_w_time: float32 [512, 512], replicated
- grad_b_time: float32 [512], replicated
- grad_ln1_gain: float32 [512], replicated
- grad_ln1_bias: float32 [512], replicated
- grad_ln2_gain: float32 [512], replicated
- grad_ln2_bias: float32 [512], replicated
- grad_b_up: float32 [2048], replicated
- grad_b_down: float32 [512], replicated
Inputs may be any that keep to these rules, and one draw needn't show every extreme that they name: `segment_ids`: never falls along a row; each document has 1 to 512 positions and one has exactly that many.
All inputs are finite; a program needn't handle non-finite values.
Results may differ from a plain program's by a relative error of at most 0.013.
Values may be sent and summed in bfloat16 or wider, within the bound.
A program may use at most 192 MiB of HBM per device.

v0:
```python
import math
import jax
import jax.numpy as jnp
from jax import lax
from jax.sharding import PartitionSpec as P

HS = 64
FF = 2048
highest = lax.Precision.HIGHEST
epsilon = 1e-05
masked_score = -1e30


def split_up(value, dim, count):
    before, after = (value.shape[:dim], value.shape[dim + 1 :])
    return jnp.moveaxis(value.reshape(*before, count, -1, *after), dim, 0)


def sent_and_summed(value, axis, dim):
    count = lax.axis_size(axis)
    parts = lax.all_to_all(split_up(value, dim, count), axis, 0, 0, tiled=True)
    return jnp.sum(parts.astype(jnp.float32), axis=0)


def side_by_side(arrays, axis, dim, along):
    ends, at = ([], 0)
    for a in arrays[:-1]:
        at += a.shape[along]
        ends.append(at)
    both = jnp.concatenate(arrays, axis=along)
    return tuple(jnp.split(sent_and_summed(both, axis, dim), ends, axis=along))


def norm_layer(values, gain_vec, shift_vec):
    row_mean = jnp.mean(values, axis=-1, keepdims=True)
    centred = values - row_mean
    variance = jnp.mean(centred * centred, axis=-1, keepdims=True)
    return centred * lax.rsqrt(variance + epsilon) * gain_vec + shift_vec


def time_features(timestep, features):
    half_width = features // 2
    frequency = jnp.exp(-math.log(10000.0) * jnp.arange(half_width, dtype=jnp.float32) / half_width)
    angles = timestep.astype(jnp.float32)[:, None] * frequency[None, :]
    return jnp.concatenate([jnp.sin(angles), jnp.cos(angles)], axis=1)


def allowed_keys(segment, length):
    places = jnp.arange(segment.shape[0], dtype=jnp.int32)
    same_doc = segment[:, None] == segment[None, :]
    is_valid = (places < length)[None, :] | (places[:, None] == places[None, :])
    return same_doc & is_valid


def gelu_tanh(values):
    return jax.nn.gelu(values, approximate=True)


def split_heads(values):
    return values.reshape(values.shape[0], values.shape[1] // HS, HS)


def head_scores(query_heads, key_heads, allowed):
    scores = jnp.einsum(
        "qhe,khe->hqk", query_heads, key_heads, preferred_element_type=jnp.float32
    ) * (1.0 / math.sqrt(HS))
    return jnp.where(allowed[None], scores, masked_score)


def attend_forward(packed):
    query_heads = split_heads(packed[0])
    key_heads = split_heads(packed[1])
    value_heads = split_heads(packed[2])
    scores = head_scores(query_heads, key_heads, allowed_keys(packed[3], packed[4]))
    row_max = jnp.max(scores, axis=-1, keepdims=True)
    raised = jnp.exp(scores - row_max)
    row_total = jnp.sum(raised, axis=-1, keepdims=True)
    probs_low = (raised / row_total).astype(jnp.bfloat16)
    mixed = jnp.einsum("hqk,khe->qhe", probs_low, value_heads, preferred_element_type=jnp.float32)
    return (mixed.reshape(packed[0].shape).astype(jnp.bfloat16), row_max + jnp.log(row_total))


def attend_backward(packed):
    query_heads = split_heads(packed[0])
    key_heads = split_heads(packed[1])
    value_heads = split_heads(packed[2])
    grad_heads = split_heads(packed[3])
    scores = head_scores(query_heads, key_heads, allowed_keys(packed[5], packed[6]))
    attn_probs = jnp.exp(scores - packed[4])
    probs_low = attn_probs.astype(jnp.bfloat16)
    grad_values = jnp.einsum(
        "hqk,qhe->khe", probs_low, grad_heads, preferred_element_type=jnp.float32
    )
    grad_probs = jnp.einsum(
        "qhe,khe->hqk", grad_heads, value_heads, preferred_element_type=jnp.float32
    )
    row_delta = jnp.sum(attn_probs * grad_probs, axis=-1, keepdims=True)
    grad_scores = (attn_probs * (grad_probs - row_delta)).astype(jnp.bfloat16)
    score_scale = 1.0 / math.sqrt(HS)
    grad_queries = (
        jnp.einsum("hqk,khe->qhe", grad_scores, key_heads, preferred_element_type=jnp.float32)
        * score_scale
    )
    grad_keys = (
        jnp.einsum("hqk,qhe->khe", grad_scores, query_heads, preferred_element_type=jnp.float32)
        * score_scale
    )
    shape_rows = packed[0].shape
    return jnp.stack(
        [
            grad_queries.reshape(shape_rows),
            grad_keys.reshape(shape_rows),
            grad_values.reshape(shape_rows),
        ]
    ).astype(jnp.bfloat16)


def shards(
    tokens,
    timestep,
    segment_ids,
    span_lengths,
    w_qkv,
    w_out_t,
    w_up,
    w_down_t,
    w_time,
    b_time,
    ln1_gain,
    ln1_bias,
    ln2_gain,
    ln2_bias,
    b_up,
    b_down,
    cotangent,
):
    tensor_place = lax.axis_index("tensor")
    qkv_copy, out_copy, up_copy, down_copy = (
        lax.all_gather(w_qkv.astype(jnp.bfloat16), "dp", axis=1, tiled=True),
        lax.all_gather(w_out_t.astype(jnp.bfloat16), "dp", axis=0, tiled=True),
        lax.all_gather(w_up.astype(jnp.bfloat16), "dp", axis=0, tiled=True),
        lax.all_gather(w_down_t.astype(jnp.bfloat16), "dp", axis=0, tiled=True),
    )
    bias_up_cols = lax.dynamic_slice_in_dim(
        b_up, tensor_place * up_copy.shape[1], up_copy.shape[1], 0
    )
    ff_cols = up_copy.shape[1]
    time_emb = time_features(timestep, tokens.shape[2])
    time_proj = jnp.dot(time_emb, w_time, precision=highest) + b_time
    start = tokens.astype(jnp.float32) + time_proj[:, None, :]
    normed_one = norm_layer(start, ln1_gain, ln1_bias).astype(jnp.bfloat16)
    normed_all = lax.all_gather(normed_one, "tensor", axis=0, tiled=True)
    qkv_act = jnp.einsum(
        "nsd,cde->cnse", normed_all, qkv_copy, preferred_element_type=jnp.float32
    ).astype(jnp.bfloat16)
    mixed, log_total = lax.map(
        attend_forward, (qkv_act[0], qkv_act[1], qkv_act[2], segment_ids, span_lengths)
    )
    part_rows = mixed
    attn_out = lax.psum_scatter(
        jnp.einsum("nse,de->nsd", part_rows, out_copy, preferred_element_type=jnp.float32),
        "tensor",
        scatter_dimension=0,
        tiled=True,
    )
    middle = start + attn_out
    normed_two = norm_layer(middle, ln2_gain, ln2_bias).astype(jnp.bfloat16)
    second_all = lax.all_gather(normed_two, "tensor", axis=0, tiled=True)
    upper = (
        jnp.einsum("nsd,df->nsf", second_all, up_copy, preferred_element_type=jnp.float32)
        + bias_up_cols
    )
    activated = gelu_tanh(upper).astype(jnp.bfloat16)
    part_rows = activated
    ffn_out = lax.psum_scatter(
        jnp.einsum("nsf,df->nsd", part_rows, down_copy, preferred_element_type=jnp.float32).astype(
            jnp.bfloat16
        ),
        "tensor",
        scatter_dimension=0,
        tiled=True,
    ).astype(jnp.float32)
    layer_out = (middle + ffn_out + b_down).astype(jnp.bfloat16)
    grad_b_down = jnp.sum(cotangent.astype(jnp.float32), axis=(0, 1))
    grad_out_all = lax.all_gather(cotangent, "tensor", axis=0, tiled=True)
    grad_down = jnp.einsum(
        "nsd,nsf->df", grad_out_all, activated, preferred_element_type=jnp.float32
    )
    grad_act = jnp.einsum(
        "nsd,df->nsf", grad_out_all, down_copy, preferred_element_type=jnp.float32
    )
    gelu_value, gelu_pull = jax.vjp(gelu_tanh, upper)
    grad_upper = gelu_pull(grad_act)[0].astype(jnp.bfloat16)
    grad_bias_cols = jnp.sum(grad_upper.astype(jnp.float32), axis=(0, 1))
    grad_up = jnp.einsum("nsd,nsf->df", second_all, grad_upper, preferred_element_type=jnp.float32)
    part_rows = grad_upper
    grad_normed_two = lax.psum_scatter(
        jnp.einsum("nsf,df->nsd", part_rows, up_copy, preferred_element_type=jnp.float32).astype(
            jnp.bfloat16
        ),
        "tensor",
        scatter_dimension=0,
        tiled=True,
    ).astype(jnp.float32)
    norm_two_value, norm_two_pull = jax.vjp(norm_layer, middle, ln2_gain, ln2_bias)
    grad_middle_norm, grad_gain_two, grad_bias_two = norm_two_pull(grad_normed_two)
    grad_middle = cotangent.astype(jnp.float32) + grad_middle_norm
    grad_attn = grad_middle.astype(jnp.bfloat16)
    grad_attn_all = lax.all_gather(grad_attn, "tensor", axis=0, tiled=True)
    grad_out_w = jnp.einsum("nsd,nse->de", grad_attn_all, mixed, preferred_element_type=jnp.float32)
    grad_mixed = jnp.einsum(
        "nsd,de->nse", grad_attn_all, out_copy, preferred_element_type=jnp.float32
    ).astype(jnp.bfloat16)
    grad_qkv_act = lax.map(
        attend_backward,
        (qkv_act[0], qkv_act[1], qkv_act[2], grad_mixed, log_total, segment_ids, span_lengths),
    )
    grad_qkv_w = jnp.einsum(
        "nsd,ncse->cde", normed_all, grad_qkv_act, preferred_element_type=jnp.float32
    )
    part_rows = grad_qkv_act
    grad_normed_one = lax.psum_scatter(
        jnp.einsum("ncse,cde->nsd", part_rows, qkv_copy, preferred_element_type=jnp.float32).astype(
            jnp.bfloat16
        ),
        "tensor",
        scatter_dimension=0,
        tiled=True,
    ).astype(jnp.float32)
    norm_one_value, norm_one_pull = jax.vjp(norm_layer, start, ln1_gain, ln1_bias)
    grad_start_norm, grad_gain_one, grad_bias_one = norm_one_pull(grad_normed_one)
    grad_tokens = grad_middle + grad_start_norm
    grad_time_rows = jnp.sum(grad_tokens, axis=1)
    grad_time_w = jnp.dot(time_emb.T, grad_time_rows, precision=highest)
    grad_time_bias = jnp.sum(grad_time_rows, axis=0)
    grad_bias_up = lax.dynamic_update_slice_in_dim(
        jnp.zeros((FF,), jnp.float32), grad_bias_cols, tensor_place * ff_cols, 0
    )
    shard_qkv, shard_out, shard_up, shard_down = (
        sent_and_summed(grad_qkv_w.astype(jnp.bfloat16), "dp", 1),
        *side_by_side(
            (
                grad_out_w.astype(jnp.bfloat16),
                grad_up.astype(jnp.bfloat16),
                grad_down.astype(jnp.bfloat16),
            ),
            "dp",
            0,
            1,
        ),
    )
    summed = lax.psum(
        (
            grad_time_w,
            grad_time_bias,
            grad_gain_one,
            grad_bias_one,
            grad_gain_two,
            grad_bias_two,
            grad_bias_up,
            grad_b_down,
        ),
        ("dp", "tensor"),
    )
    return (
        layer_out,
        grad_tokens,
        shard_qkv,
        shard_out,
        shard_up,
        shard_down,
        summed[0],
        summed[1],
        summed[2],
        summed[3],
        summed[4],
        summed[5],
        summed[6],
        summed[7],
    )


def solution(mesh):
    return jax.shard_map(
        shards,
        mesh=mesh,
        in_specs=(
            P(("dp", "tensor"), None, None),
            P(("dp", "tensor")),
            P("dp", None),
            P("dp"),
            P(None, "dp", "tensor"),
            P("dp", "tensor"),
            P("dp", "tensor"),
            P("dp", "tensor"),
            P(),
            P(),
            P(),
            P(),
            P(),
            P(),
            P(),
            P(),
            P(("dp", "tensor"), None, None),
        ),
        out_specs=(
            P(("dp", "tensor"), None, None),
            P(("dp", "tensor"), None, None),
            P(None, "dp", "tensor"),
            P("dp", "tensor"),
            P("dp", "tensor"),
            P("dp", "tensor"),
            P(),
            P(),
            P(),
            P(),
            P(),
            P(),
            P(),
            P(),
        ),
        check_vma=False,
    )
```

profile of v0, /device:TPU:0, one launch (start us, length us, event | category | flops | bytes accessed | tf_op | source)
XLA Modules:
  0.0 1040.7 jit_solution(14734776910179383602)
XLA Ops:
  15.9 10.7 %all_gather.26 = bf16[512,128]{1,0:T(8,128)(2,1)S(1)} all-gather(bf16[64,128]{1,0:T(8,128)(2,1)S(1)} %convert_element_type.133), channel_id=1, replica_groups=mesh['dp'=8,'tensor'=4] {'dp'}, dimensions={0}, use_global_device_ids=true | all-gather | bytes 147456 | tf_op jit(solution)/shard_map/all_gather | solution.py:140
  26.6 9.7 all_gather.25
  36.3 63.1 %all-gather.5.cloned.1.call-done = bf16[4,1024,512]{2,1,0:T(8,128)(2,1)} async-done(((bf16[1,1024,512]{2,1,0:T(8,128)(2,1)}), bf16[4,1024,512]{2,1,0:T(8,128)(2,1)}) %all-gather.5.cloned.1.call-update) | async-done | bytes 4194320 | tf_op jit(solution)/shard_map/all_gather | solution.py:152
  109.8 42.4 %while.22 = (s32[]{:T(128)}, bf16[4,1024,128]{1,2,0:T(8,128)(2,1)S(1)}, f32[4,2,1024,1]{2,1,3,0:T(2,128)S(1)}, bf16[4,1024,128]{1,2,0:T(8,128)(2,1)S(1)}, s32[4,...) while((s32[]{:T(128)}, ...), condition=%wide.region_5.6_spmd, body=%wide.region_2.5_spmd.sunk | while | flops 566361088 | bytes 32585864 | solution.py:156
  156.9 143.1 %reduce-scatter.5.cloned.1.call-done = f32[1,1024,512]{2,1,0:T(8,128)} async-done(((f32[4,1024,512]{2,1,0:T(8,128)}), f32[1,1024,512]{2,1,0:T(8,128)}) %reduce-scatter.5.cloned.1.call-update) | async-done | bytes 2097168 | tf_op jit(solution)/shard_map/reduce_scatter | solution.py:160
  305.2 10.2 all_gather.29
  315.4 9.8 all_gather.28
  325.2 60.2 %all-gather.7.cloned.1.call-done = bf16[4,1024,512]{2,1,0:T(8,128)(2,1)} async-done(((bf16[1,1024,512]{2,1,0:T(8,128)(2,1)}), bf16[4,1024,512]{2,1,0:T(8,128)(2,1)}) %all-gather.7.cloned.1.call-update) | async-done | bytes 4194320 | tf_op jit(solution)/shard_map/all_gather | solution.py:168
  385.5 8.0 fusion.64
  393.4 72.8 %all-gather.9.cloned.1.call-done = bf16[4,1024,512]{2,1,0:T(8,128)(2,1)} async-done(((bf16[1,1024,512]{2,1,0:T(8,128)(2,1)}), bf16[4,1024,512]{2,1,0:T(8,128)(2,1)}) %all-gather.9.cloned.1.call-update) | async-done | bytes 4194320 | tf_op jit(solution)/shard_map/all_gather | solution.py:185
  466.2 10.3 convert_reduce_fusion
  483.1 8.8 convolution_convert_fusion.1
  491.9 66.5 %reduce-scatter.9.cloned.1.call-done = bf16[1,1024,512]{2,1,0:T(8,128)(2,1)} async-done(((bf16[4,1024,512]{2,1,0:T(8,128)(2,1)}), bf16[1,1024,512]{2,1,0:T(8,128)(2,1)}) %reduce-scatter.9.cloned.1.call-update) | async-done | bytes 1048592 | tf_op jit(solution)/shard_map/reduce_scatter | solution.py:197
  561.2 76.8 %reduce-scatter.7.cloned.1.call-done = bf16[1,1024,512]{2,1,0:T(8,128)(2,1)} async-done(((bf16[4,1024,512]{2,1,0:T(8,128)(2,1)}), bf16[1,1024,512]{2,1,0:T(8,128)(2,1)}) %reduce-scatter.7.cloned.1.call-update) | async-done | bytes 1048592 | tf_op jit(solution)/shard_map/reduce_scatter | solution.py:175
  644.2 81.2 %all-gather.11.cloned.1.call-done = bf16[4,1024,512]{2,1,0:T(8,128)(2,1)} async-done(((bf16[1,1024,512]{2,1,0:T(8,128)(2,1)}), bf16[4,1024,512]{2,1,0:T(8,128)(2,1)}) %all-gather.11.cloned.1.call-update) | async-done | bytes 4194320 | tf_op jit(solution)/shard_map/all_gather | solution.py:209
  728.8 72.6 %while.23 = (s32[]{:T(128)}, bf16[4,3,1024,128]{2,3,1,0:T(8,128)(2,1)}, bf16[4,1024,128]{1,2,0:T(8,128)(2,1)}, s32[4,1024]{1,0:T(4,128)S(1)}, s32[4]{0:T(128)S(1...) while((s32[]{:T(128)}, ...), condition=%wide.region_15.16_spmd, body=%wide.region_13.15_spmd.sunk | while | flops 1380842496 | bytes 73996440 | solution.py:214
  801.4 6.3 bitcast_convert_fusion
  809.3 6.5 fusion.47
  815.9 7.1 fusion.55
  825.3 5.1 fusion.57
  835.2 47.9 %reduce-scatter.11.cloned.1.call-done = bf16[1,1024,512]{2,1,0:T(8,128)(2,1)} async-done(((bf16[4,1024,512]{2,1,0:T(8,128)(2,1)}), bf16[1,1024,512]{2,1,0:T(8,128)(2,1)}) %reduce-scatter.11.cloned.1.call-update) | async-done | bytes 1048592 | tf_op jit(solution)/shard_map/reduce_scatter | solution.py:222
  900.1 10.1 all-to-all-done.1
  913.0 41.1 %all-reduce = (f32[512]{0:T(512)}, f32[512]{0:T(512)}, f32[512]{0:T(512)}, f32[512]{0:T(512)}, f32[512]{0:T(512)}, /*index=5*/f32[2048]{0:T(1024)}, f32[512]{0:T(512)}) all-reduce(f32[512]{0:T(512)} %copy-done.32, f32[512]{0:T(512)S(1)} %copy-done.38, f32[512]{0:T(512)S(1)} %copy-done.37, ...), channel_id=1, replica_groups=mesh['dp'=8,'tensor'=4] {'dp','tensor'}, use_global_device_ids=true, to_apply=%region_23.24 | all-reduce | flops 5120 | bytes 40960 | tf_op jit(solution)/shard_map/psum | solution.py:252
  954.1 77.5 %all-reduce.3.cloned.1.call-done = f32[512,512]{1,0:T(8,128)} async-done(((f32[512,512]{1,0:T(8,128)}), f32[512,512]{1,0:T(8,128)}) %all-reduce.3.cloned.1.call-update) | async-done | bytes 1048592 | tf_op jit(solution)/shard_map/psum | solution.py:252
  (278 shorter events, 191.8 us)
Async XLA Ops:
  7.2 92.1 %all-gather.5.cloned.1.call-start = ((), (), s32[]{:S(2)}) async-start(), calls=%async_computation.6 | async-start | bytes 5242880 | tf_op jit(solution)/shard_map/all_gather | solution.py:152
  9.7 290.2 %copy-start.18 = (f32[512]{0:T(512)}, f32[512]{0:T(512)S(1)}, u32[]{:S(2)}) copy-start(f32[512]{0:T(512)S(1)} %add.138) | copy-start | bytes 6148
  15.7 284.2 %reduce-scatter.5.cloned.1.call-start = ((), (), s32[]{:S(2)}) async-start(), calls=%async_computation.7 | async-start | bytes 10485760 | tf_op jit(solution)/shard_map/reduce_scatter | solution.py:160
  36.3 67.6 %copy-start.12 = (bf16[3,512,128]{2,1,0:T(8,128)(2,1)}, bf16[3,512,128]{2,1,0:T(8,128)(2,1)S(1)}, u32[]{:S(2)}) copy-start(bf16[3,512,128]{2,1,0:T(8,128)(2,1)S(1)} %all_gather.25) | copy-start | bytes 1179652
  156.8 143.2 %copy-start.2 = (bf16[1,1024,512]{2,1,0:T(8,128)(2,1)S(1)}, bf16[1,1024,512]{2,1,0:T(8,128)(2,1)}, u32[]{:S(2)}) copy-start(bf16[1,1024,512]{2,1,0:T(8,128)(2,1)} %param.21) | copy-start | bytes 3145732
  156.8 145.5 %copy-start.31 = (f32[512]{0:T(512)S(1)}, f32[512]{0:T(512)}, u32[]{:S(2)}) copy-start(f32[512]{0:T(512)} %param.33) | copy-start | bytes 6148
  156.8 145.5 %copy-start.43 = (f32[512]{0:T(512)S(1)}, f32[512]{0:T(512)}, u32[]{:S(2)}) copy-start(f32[512]{0:T(512)} %param.34) | copy-start | bytes 6148
  156.8 228.6 %all-gather.7.cloned.1.call-start = ((), (), s32[]{:S(2)}) async-start(), calls=%async_computation.8 | async-start | bytes 5242880 | tf_op jit(solution)/shard_map/all_gather | solution.py:168
  303.7 162.5 %all-gather.9.cloned.1.call-start = ((), (), s32[]{:S(2)}) async-start(), calls=%async_computation.10 | async-start | bytes 5242880 | tf_op jit(solution)/shard_map/all_gather | solution.py:185
  304.3 254.1 %reduce-scatter.9.cloned.1.call-start = ((), (), s32[]{:S(2)}) async-start(), calls=%async_computation.11 | async-start | bytes 5242880 | tf_op jit(solution)/shard_map/reduce_scatter | solution.py:197
  483.0 155.0 %reduce-scatter.7.cloned.1.call-start = ((), (), s32[]{:S(2)}) async-start(), calls=%async_computation.9 | async-start | bytes 5242880 | tf_op jit(solution)/shard_map/reduce_scatter | solution.py:175
  491.8 146.2 %copy-start.44 = (f32[512]{0:T(512)S(1)}, f32[512]{0:T(512)}, u32[]{:S(2)}) copy-start(f32[512]{0:T(512)} %param.36) | copy-start | bytes 6148
  491.9 233.5 %all-gather.11.cloned.1.call-start = ((), (), s32[]{:S(2)}) async-start(), calls=%async_computation.12 | async-start | bytes 5242880 | tf_op jit(solution)/shard_map/all_gather | solution.py:209
  561.2 81.3 %copy-start.8 = (bf16[1,1024,512]{2,1,0:T(8,128)(2,1)S(1)}, bf16[1,1024,512]{2,1,0:T(8,128)(2,1)}, u32[]{:S(2)}) copy-start(bf16[1,1024,512]{2,1,0:T(8,128)(2,1)} %param.37) | copy-start | bytes 3145732
  641.2 87.6 %copy-start.24 = (f32[1024]{0:T(1024)}, f32[1024]{0:T(1024)S(1)}, u32[]{:S(2)}) copy-start(f32[1024]{0:T(1024)S(1)} %negate_multiply_fusion.1) | copy-start | bytes 12292
  643.9 239.2 %reduce-scatter.11.cloned.1.call-start = ((), (), s32[]{:S(2)}) async-start(), calls=%async_computation.13 | async-start | bytes 5242880 | tf_op jit(solution)/shard_map/reduce_scatter | solution.py:222
  728.8 72.6 %copy-start.13 = (bf16[3,512,128]{2,1,0:T(8,128)(2,1)S(1)}, bf16[3,512,128]{2,1,0:T(8,128)(2,1)}, u32[]{:S(2)}) copy-start(bf16[3,512,128]{2,1,0:T(8,128)(2,1)} %copy-done.12) | copy-start | bytes 1179652
  825.3 57.9 %copy-start.19 = (f32[512]{0:T(512)S(1)}, f32[512]{0:T(512)}, u32[]{:S(2)}) copy-start(f32[512]{0:T(512)} %copy-done.18) | copy-start | bytes 6148
  825.3 57.9 %copy-start.30 = (f32[512]{0:T(512)S(1)}, f32[512]{0:T(512)}, u32[]{:S(2)}) copy-start(f32[512]{0:T(512)} %param.31) | copy-start | bytes 6148
  830.7 62.7 %copy-start.9 = (bf16[1,1024,512]{2,1,0:T(8,128)(2,1)S(1)}, bf16[1,1024,512]{2,1,0:T(8,128)(2,1)}, u32[]{:S(2)}) copy-start(bf16[1,1024,512]{2,1,0:T(8,128)(2,1)} %param.37) | copy-start | bytes 3145732
  831.4 57.5 %all-to-all-start = ((bf16[8,3,64,128]{3,2,1,0:T(8,128)(2,1)}), bf16[8,3,64,128]{3,2,1,0:T(8,128)(2,1)S(1)}, u32[]{:S(2)}, u32[]{:S(2)}) async-start(bf16[8,3,64,128]{3,2,1,0:T(8,128)(2,1)} %copy.79), calls=%async_computation.4 | async-start | bytes 786432 | tf_op jit(solution)/shard_map/all_to_all | solution.py:21
  889.0 21.2 %all-to-all-start.1 = ((bf16[8,64,1152]{2,1,0:T(8,128)(2,1)}), bf16[8,64,1152]{2,1,0:T(8,128)(2,1)}, u32[]{:S(2)}, u32[]{:S(2)}) async-start(bf16[8,64,1152]{2,1,0:T(8,128)(2,1)} %bitcast.206), calls=%async_computation.5 | async-start | bytes 2359296 | tf_op jit(solution)/shard_map/all_to_all | solution.py:21
  893.2 138.4 %all-reduce.3.cloned.1.call-start = ((), (), s32[]{:S(2)}) async-start(), calls=%async_computation.14 | async-start | bytes 2097152 | tf_op jit(solution)/shard_map/psum | solution.py:252
  893.3 140.6 %copy-start.1 = (f32[512,512]{1,0:T(8,128)S(1)}, f32[512,512]{1,0:T(8,128)}, u32[]{:S(2)}) copy-start(f32[512,512]{1,0:T(8,128)} %param.29) | copy-start | bytes 3145732
  (35 other events, 421.4 us)
Sparse Core Ops, SparseCore 0:
  15.9 83.4 all-gather.4
  156.9 142.9 reduce-scatter.4
  303.9 81.5 all-gather.6
  386.9 79.2 all-gather.8
  483.1 75.2 reduce-scatter.8
  560.7 77.2 reduce-scatter.6
  644.0 81.2 all-gather.10
  807.8 75.2 reduce-scatter.10
  900.7 130.9 all-reduce.2
where the time goes:
time: 1040 us
  waiting for transfers between devices  700 us (67%)
  matrix products  127 us (12%)
  blocking collectives  81.5 us (8%)
  other arithmetic  71.6 us (7%)
  local copies, waits for them, and re-layouts  35.8 us (3%)
  between operations  15.5 us (1%)
    reduce_scatter x1, waiting for transfers between devices, shards(): lax.psum_scatter(jnp.einsum('nse,de->nsd', part_rows, out_copy, preferred...  143 us
    all_gather x1, waiting for transfers between devices, shards(): grad_attn_all = lax.all_gather(grad_attn, 'tensor', axis=0, tiled=True)  81.2 us
    psum x1, waiting for transfers between devices, shards(): lax.psum((grad_time_w, grad_time_bias, grad_gain_one, grad_bias_one, grad...  77.5 us
    reduce_scatter x1, waiting for transfers between devices, shards(): lax.psum_scatter(jnp.einsum('nsf,df->nsd', part_rows, down_copy, preferre...  76.8 us
    all_gather x1, waiting for transfers between devices, shards(): grad_out_all = lax.all_gather(cotangent, 'tensor', axis=0, tiled=True)  72.8 us
    reduce_scatter x1, waiting for transfers between devices, shards(): lax.psum_scatter(jnp.einsum('nsf,df->nsd', part_rows, up_copy, preferred_...  66.5 us
    all_gather x1, waiting for transfers between devices, shards(): normed_all = lax.all_gather(normed_one, 'tensor', axis=0, tiled=True)  63.1 us
    all_gather x1, waiting for transfers between devices, shards(): second_all = lax.all_gather(normed_two, 'tensor', axis=0, tiled=True)  60.2 us
  transfers between devices with their start and end apart: 11, of which 10 were waited for; matrix products, arithmetic and copies ran while one was open for 6% of the time, Pallas kernels for 0%

commit v1 on v0

--- a/solution.py
+++ b/solution.py
@@ -250,17 +250,20 @@
         ),
     )
     summed = lax.psum(
-        (
-            grad_time_w,
-            grad_time_bias,
-            grad_gain_one,
-            grad_bias_one,
-            grad_gain_two,
-            grad_bias_two,
-            grad_bias_up,
-            grad_b_down,
-        ),
-        ("dp", "tensor"),
+        lax.psum(
+            (
+                grad_time_w,
+                grad_time_bias,
+                grad_gain_one,
+                grad_bias_one,
+                grad_gain_two,
+                grad_bias_two,
+                grad_bias_up,
+                grad_b_down,
+            ),
+            "tensor",
+        ),
+        "dp",
     )
     return (
         layer_out,

time: 1040 us -> 1020 us (0.981)
  waiting for transfers between devices: 700 us -> 675 us
    psum x1, waiting for transfers between devices: 77.5 us -> 45.7 us  [shards(): lax.psum((grad_time_w, grad_time_bias, grad_gain_one, grad_bias_one, grad...]
    psum x1, blocking collectives: 41.1 us -> 17.5 us  [shards(): lax.psum((grad_time_w, grad_time_bias, grad_gain_one, grad_bias_one, grad...]
    psum x0 -> x1, blocking collectives: none -> 23 us  [shards(): lax.psum(lax.psum((grad_time_w, grad_time_bias, grad_gain_one, grad_bias_...]
    psum x0 -> x1, waiting for transfers between devices: none -> 16.3 us  [shards(): lax.psum(lax.psum((grad_time_w, grad_time_bias, grad_gain_one, grad_bias_...]
  transfers between devices with their start and end apart: 11 -> 12, of which waited for: 10 -> 10; matrix products, arithmetic and copies ran while one was open for 6% -> 6% of each run, Pallas kernels for 0% -> 0%
where the time goes in v1:
time: 1020 us
  waiting for transfers between devices  675 us (66%)
  matrix products  129 us (13%)
  blocking collectives  80.8 us (8%)
  other arithmetic  71.8 us (7%)
  local copies, waits for them, and re-layouts  35.2 us (3%)
  between operations  15.8 us (2%)
    reduce_scatter x1, waiting for transfers between devices, shards(): lax.psum_scatter(jnp.einsum('nse,de->nsd', part_rows, out_copy, preferred...  143 us
    all_gather x1, waiting for transfers between devices, shards(): grad_attn_all = lax.all_gather(grad_attn, 'tensor', axis=0, tiled=True)  80.9 us
    reduce_scatter x1, waiting for transfers between devices, shards(): lax.psum_scatter(jnp.einsum('nsf,df->nsd', part_rows, down_copy, preferre...  76.8 us
    all_gather x1, waiting for transfers between devices, shards(): grad_out_all = lax.all_gather(cotangent, 'tensor', axis=0, tiled=True)  72.8 us
    reduce_scatter x1, waiting for transfers between devices, shards(): lax.psum_scatter(jnp.einsum('nsf,df->nsd', part_rows, up_copy, preferred_...  66.6 us
    all_gather x1, waiting for transfers between devices, shards(): normed_all = lax.all_gather(normed_one, 'tensor', axis=0, tiled=True)  63.1 us
    all_gather x1, waiting for transfers between devices, shards(): second_all = lax.all_gather(normed_two, 'tensor', axis=0, tiled=True)  60.4 us
    reduce_scatter x1, waiting for transfers between devices, shards(): lax.psum_scatter(jnp.einsum('ncse,cde->nsd', part_rows, qkv_copy, preferr...  49.1 us
  transfers between devices with their start and end apart: 12, of which 10 were waited for; matrix products, arithmetic and copies ran while one was open for 6% of the time, Pallas kernels for 0%

profile of v1, /device:TPU:0, one launch (start us, length us, event | category | flops | bytes accessed | tf_op | source)
XLA Modules:
  0.0 1016.9 jit_solution(5509889310444060920)
XLA Ops:
  15.9 10.7 %all_gather.26 = bf16[512,128]{1,0:T(8,128)(2,1)S(1)} all-gather(bf16[64,128]{1,0:T(8,128)(2,1)S(1)} %convert_element_type.133), channel_id=1, replica_groups=mesh['dp'=8,'tensor'=4] {'dp'}, dimensions={0}, use_global_device_ids=true | all-gather | bytes 147456 | tf_op jit(solution)/shard_map/all_gather | solution.py:140
  26.6 9.7 all_gather.25
  36.3 63.1 %all-gather.5.cloned.1.call-done = bf16[4,1024,512]{2,1,0:T(8,128)(2,1)} async-done(((bf16[1,1024,512]{2,1,0:T(8,128)(2,1)}), bf16[4,1024,512]{2,1,0:T(8,128)(2,1)}) %all-gather.5.cloned.1.call-update) | async-done | bytes 4194320 | tf_op jit(solution)/shard_map/all_gather | solution.py:152
  109.8 42.4 %while.22 = (s32[]{:T(128)}, bf16[4,1024,128]{1,2,0:T(8,128)(2,1)S(1)}, f32[4,2,1024,1]{2,1,3,0:T(2,128)S(1)}, bf16[4,1024,128]{1,2,0:T(8,128)(2,1)S(1)}, s32[4,...) while((s32[]{:T(128)}, ...), condition=%wide.region_5.6_spmd, body=%wide.region_2.5_spmd.sunk | while | flops 566361088 | bytes 32585864 | solution.py:156
  156.9 143.1 %reduce-scatter.5.cloned.1.call-done = f32[1,1024,512]{2,1,0:T(8,128)} async-done(((f32[4,1024,512]{2,1,0:T(8,128)}), f32[1,1024,512]{2,1,0:T(8,128)}) %reduce-scatter.5.cloned.1.call-update) | async-done | bytes 2097168 | tf_op jit(solution)/shard_map/reduce_scatter | solution.py:160
  305.2 10.0 all_gather.29
  315.2 9.8 all_gather.28
  325.0 60.4 %all-gather.7.cloned.1.call-done = bf16[4,1024,512]{2,1,0:T(8,128)(2,1)} async-done(((bf16[1,1024,512]{2,1,0:T(8,128)(2,1)}), bf16[4,1024,512]{2,1,0:T(8,128)(2,1)}) %all-gather.7.cloned.1.call-update) | async-done | bytes 4194320 | tf_op jit(solution)/shard_map/all_gather | solution.py:168
  385.4 8.0 fusion.64
  393.4 72.8 %all-gather.9.cloned.1.call-done = bf16[4,1024,512]{2,1,0:T(8,128)(2,1)} async-done(((bf16[1,1024,512]{2,1,0:T(8,128)(2,1)}), bf16[4,1024,512]{2,1,0:T(8,128)(2,1)}) %all-gather.9.cloned.1.call-update) | async-done | bytes 4194320 | tf_op jit(solution)/shard_map/all_gather | solution.py:185
  466.2 10.8 %convert_reduce_fusion = (f32[512]{0:T(512)}, bf16[4,1024,512]{2,1,0:T(8,128)(2,1)S(1)}) fusion(f32[4,1024,512]{2,1,0:T(8,128)} %fusion.64, f32[512]{0:T(512)S(1)} %dynamic_slice.43, bf16[4,1024,512]{2,1,0:T(8,128)(2,1)} %all-gather.9.cloned.1.call-done, bf16[512,512]{1,0:T(8,128)(2,1)S(1)} %all_gather.29), kind=kOutput, calls=%fused_computation.53 | convolution fusion | flops 2195717632 | bytes 17305600 | tf_op jit(solution)/shard_map/nsd,df->nsf/dot_general | solution.py:189
  483.6 8.8 convolution_convert_fusion.1
  492.4 66.6 %reduce-scatter.9.cloned.1.call-done = bf16[1,1024,512]{2,1,0:T(8,128)(2,1)} async-done(((bf16[4,1024,512]{2,1,0:T(8,128)(2,1)}), bf16[1,1024,512]{2,1,0:T(8,128)(2,1)}) %reduce-scatter.9.cloned.1.call-update) | async-done | bytes 1048592 | tf_op jit(solution)/shard_map/reduce_scatter | solution.py:197
  561.7 76.8 %reduce-scatter.7.cloned.1.call-done = bf16[1,1024,512]{2,1,0:T(8,128)(2,1)} async-done(((bf16[4,1024,512]{2,1,0:T(8,128)(2,1)}), bf16[1,1024,512]{2,1,0:T(8,128)(2,1)}) %reduce-scatter.7.cloned.1.call-update) | async-done | bytes 1048592 | tf_op jit(solution)/shard_map/reduce_scatter | solution.py:175
  644.9 80.9 %all-gather.11.cloned.1.call-done = bf16[4,1024,512]{2,1,0:T(8,128)(2,1)} async-done(((bf16[1,1024,512]{2,1,0:T(8,128)(2,1)}), bf16[4,1024,512]{2,1,0:T(8,128)(2,1)}) %all-gather.11.cloned.1.call-update) | async-done | bytes 4194320 | tf_op jit(solution)/shard_map/all_gather | solution.py:209
  729.3 72.7 %while.23 = (s32[]{:T(128)}, bf16[4,3,1024,128]{2,3,1,0:T(8,128)(2,1)}, bf16[4,1024,128]{1,2,0:T(8,128)(2,1)}, s32[4,1024]{1,0:T(4,128)S(1)}, s32[4]{0:T(128)S(1...) while((s32[]{:T(128)}, ...), condition=%wide.region_15.16_spmd, body=%wide.region_13.15_spmd.sunk | while | flops 1380842496 | bytes 73996440 | solution.py:214
  802.1 6.2 bitcast_convert_fusion
  809.0 6.8 fusion.47
  815.7 8.4 fusion.55
  834.8 49.1 %reduce-scatter.11.cloned.1.call-done = bf16[1,1024,512]{2,1,0:T(8,128)(2,1)} async-done(((bf16[4,1024,512]{2,1,0:T(8,128)(2,1)}), bf16[1,1024,512]{2,1,0:T(8,128)(2,1)}) %reduce-scatter.11.cloned.1.call-update) | async-done | bytes 1048592 | tf_op jit(solution)/shard_map/reduce_scatter | solution.py:222
  902.8 45.7 %all-reduce.5.cloned.1.call-done = f32[512,512]{1,0:T(8,128)} async-done(((f32[512,512]{1,0:T(8,128)}), f32[512,512]{1,0:T(8,128)}) %all-reduce.5.cloned.1.call-update) | async-done | bytes 1048592 | tf_op jit(solution)/shard_map/psum | solution.py:253
  950.7 17.5 %all-reduce.1 = (f32[512]{0:T(512)S(1)}, f32[512]{0:T(512)S(1)}, f32[512]{0:T(512)S(1)}, f32[512]{0:T(512)S(1)}, f32[512]{0:T(512)S(1)}, /*index=5*/f32[2048]{0:T(1024)S(1)}, f32[512]{0:T(512)S(1)}) all-reduce(f32[512]{0:T(512)S(1)} %copy-done.28, f32[512]{0:T(512)S(1)} %copy-done.34, ...), channel_id=1, replica_groups=mesh['dp'=8,'tensor'=4] {'tensor'}, use_global_device_ids=true, to_apply=%region_24.25 | all-reduce | flops 5120 | bytes 40960 | tf_op jit(solution)/shard_map/psum | solution.py:253
  968.3 23.0 %all-reduce = (f32[512]{0:T(512)}, f32[512]{0:T(512)}, f32[512]{0:T(512)}, f32[512]{0:T(512)}, f32[512]{0:T(512)}, /*index=5*/f32[2048]{0:T(1024)}, f32[512]{0:T(512)}) all-reduce(f32[512]{0:T(512)S(1)} %get-tuple-element.206, f32[512]{0:T(512)S(1)} %get-tuple-element.207, ...), channel_id=1, replica_groups=mesh['dp'=8,'tensor'=4] {'dp'}, use_global_device_ids=true, to_apply=%region_25.26 | all-reduce | flops 5120 | bytes 40960 | tf_op jit(solution)/shard_map/psum | solution.py:252
  991.3 16.3 %all-reduce.7.cloned.1.call-done = f32[512,512]{1,0:T(8,128)} async-done(((f32[512,512]{1,0:T(8,128)}), f32[512,512]{1,0:T(8,128)}) %all-reduce.7.cloned.1.call-update) | async-done | bytes 1048592 | tf_op jit(solution)/shard_map/psum | solution.py:252
  (280 shorter events, 195.9 us)
Async XLA Ops:
  7.2 92.1 %all-gather.5.cloned.1.call-start = ((), (), s32[]{:S(2)}) async-start(), calls=%async_computation.6 | async-start | bytes 5242880 | tf_op jit(solution)/shard_map/all_gather | solution.py:152
  9.7 290.2 %copy-start.18 = (f32[512]{0:T(512)}, f32[512]{0:T(512)S(1)}, u32[]{:S(2)}) copy-start(f32[512]{0:T(512)S(1)} %add.154) | copy-start | bytes 6148
  15.7 284.2 %reduce-scatter.5.cloned.1.call-start = ((), (), s32[]{:S(2)}) async-start(), calls=%async_computation.7 | async-start | bytes 10485760 | tf_op jit(solution)/shard_map/reduce_scatter | solution.py:160
  36.3 67.6 %copy-start.12 = (bf16[3,512,128]{2,1,0:T(8,128)(2,1)}, bf16[3,512,128]{2,1,0:T(8,128)(2,1)S(1)}, u32[]{:S(2)}) copy-start(bf16[3,512,128]{2,1,0:T(8,128)(2,1)S(1)} %all_gather.25) | copy-start | bytes 1179652
  156.7 143.2 %copy-start.2 = (bf16[1,1024,512]{2,1,0:T(8,128)(2,1)S(1)}, bf16[1,1024,512]{2,1,0:T(8,128)(2,1)}, u32[]{:S(2)}) copy-start(bf16[1,1024,512]{2,1,0:T(8,128)(2,1)} %param.21) | copy-start | bytes 3145732
  156.8 145.5 %copy-start.26 = (f32[512]{0:T(512)S(1)}, f32[512]{0:T(512)}, u32[]{:S(2)}) copy-start(f32[512]{0:T(512)} %param.33) | copy-start | bytes 6148
  156.8 145.5 %copy-start.39 = (f32[512]{0:T(512)S(1)}, f32[512]{0:T(512)}, u32[]{:S(2)}) copy-start(f32[512]{0:T(512)} %param.34) | copy-start | bytes 6148
  156.8 228.6 %all-gather.7.cloned.1.call-start = ((), (), s32[]{:S(2)}) async-start(), calls=%async_computation.8 | async-start | bytes 5242880 | tf_op jit(solution)/shard_map/all_gather | solution.py:168
  303.7 162.5 %all-gather.9.cloned.1.call-start = ((), (), s32[]{:S(2)}) async-start(), calls=%async_computation.10 | async-start | bytes 5242880 | tf_op jit(solution)/shard_map/all_gather | solution.py:185
  304.3 254.7 %reduce-scatter.9.cloned.1.call-start = ((), (), s32[]{:S(2)}) async-start(), calls=%async_computation.11 | async-start | bytes 5242880 | tf_op jit(solution)/shard_map/reduce_scatter | solution.py:197
  483.5 155.0 %reduce-scatter.7.cloned.1.call-start = ((), (), s32[]{:S(2)}) async-start(), calls=%async_computation.9 | async-start | bytes 5242880 | tf_op jit(solution)/shard_map/reduce_scatter | solution.py:175
  492.4 146.2 %copy-start.40 = (f32[512]{0:T(512)S(1)}, f32[512]{0:T(512)}, u32[]{:S(2)}) copy-start(f32[512]{0:T(512)} %param.36) | copy-start | bytes 6148
  492.4 233.5 %all-gather.11.cloned.1.call-start = ((), (), s32[]{:S(2)}) async-start(), calls=%async_computation.12 | async-start | bytes 5242880 | tf_op jit(solution)/shard_map/all_gather | solution.py:209
  561.7 81.3 %copy-start.8 = (bf16[1,1024,512]{2,1,0:T(8,128)(2,1)S(1)}, bf16[1,1024,512]{2,1,0:T(8,128)(2,1)}, u32[]{:S(2)}) copy-start(bf16[1,1024,512]{2,1,0:T(8,128)(2,1)} %param.37) | copy-start | bytes 3145732
  644.5 239.4 %reduce-scatter.11.cloned.1.call-start = ((), (), s32[]{:S(2)}) async-start(), calls=%async_computation.13 | async-start | bytes 5242880 | tf_op jit(solution)/shard_map/reduce_scatter | solution.py:222
  729.3 72.8 %copy-start.13 = (bf16[3,512,128]{2,1,0:T(8,128)(2,1)S(1)}, bf16[3,512,128]{2,1,0:T(8,128)(2,1)}, u32[]{:S(2)}) copy-start(bf16[3,512,128]{2,1,0:T(8,128)(2,1)} %copy-done.12) | copy-start | bytes 1179652
  826.9 71.8 %all-to-all-start = ((bf16[8,3,64,128]{3,2,1,0:T(8,128)(2,1)}), bf16[8,3,64,128]{3,2,1,0:T(8,128)(2,1)S(1)}, u32[]{:S(2)}, u32[]{:S(2)}) async-start(bf16[8,3,64,128]{3,2,1,0:T(8,128)(2,1)} %copy.79), calls=%async_computation.4 | async-start | bytes 786432 | tf_op jit(solution)/shard_map/all_to_all | solution.py:21
  830.7 56.7 %copy-start.23 = (f32[1024]{0:T(1024)S(1)}, f32[1024]{0:T(1024)}, u32[]{:S(2)}) copy-start(f32[1024]{0:T(1024)} %copy-done.22) | copy-start | bytes 12292
  830.7 60.0 %copy-start.5 = (f32[1,1024,512]{2,1,0:T(8,128)S(1)}, f32[1,1024,512]{2,1,0:T(8,128)}, u32[]{:S(2)}) copy-start(f32[1,1024,512]{2,1,0:T(8,128)} %copy-done.4) | copy-start | bytes 6291460
  830.7 117.8 %all-reduce.5.cloned.1.call-start = ((), (), s32[]{:S(2)}) async-start(), calls=%async_computation.14 | async-start | bytes 2097152 | tf_op jit(solution)/shard_map/psum | solution.py:253
  897.3 53.4 %copy-start.28 = (f32[512]{0:T(512)S(1)}, f32[512]{0:T(512)}, u32[]{:S(2)}) copy-start(f32[512]{0:T(512)} %copy-done.27) | copy-start | bytes 6148
  897.4 112.5 %copy-start.1 = (f32[512,512]{1,0:T(8,128)S(1)}, f32[512,512]{1,0:T(8,128)}, u32[]{:S(2)}) copy-start(f32[512,512]{1,0:T(8,128)} %param.29) | copy-start | bytes 3145732
  898.8 50.4 %all-to-all-start.1 = ((bf16[8,64,1152]{2,1,0:T(8,128)(2,1)}), bf16[8,64,1152]{2,1,0:T(8,128)(2,1)S(1)}, u32[]{:S(2)}, u32[]{:S(2)}) async-start(bf16[8,64,1152]{2,1,0:T(8,128)(2,1)} %bitcast.46), calls=%async_computation.5 | async-start | bytes 2359296 | tf_op jit(solution)/shard_map/all_to_all | solution.py:21
  902.4 105.1 %all-reduce.7.cloned.1.call-start = ((), (), s32[]{:S(2)}) async-start(), calls=%async_computation.15 | async-start | bytes 2097152 | tf_op jit(solution)/shard_map/psum | solution.py:252
  (35 other events, 551.2 us)
Sparse Core Ops, SparseCore 0:
  15.9 83.4 all-gather.4
  156.9 142.9 reduce-scatter.4
  303.8 81.5 all-gather.6
  386.9 79.2 all-gather.8
  483.6 75.2 reduce-scatter.8
  561.2 77.2 reduce-scatter.6
  644.6 81.2 all-gather.10
  808.5 75.2 reduce-scatter.10
  896.1 52.3 all-reduce.4
  951.5 56.0 all-reduce.6
